TPU v7x, 32 devices: a whole 2x2x4 slice. The times are simulated.
32 devices in a mesh: dx: 4 (over y, core), dy: 4 (over z), band: 2 (over x).
Axes of the slice: x: 2, y: 2, z: 4, core: 2. Of those that a mesh axis runs over, the one named last changes fastest.
Arguments:
- states: float32 [24, 32, 8, 512], P('dx', 'dy', None, 'band'), may hold values from -6 to 6
- potential: float32 [24, 32, 8], P('dx', 'dy'), may hold values from -1 to 1
Outputs:
- orthonormal: float32 [24, 32, 8, 512], P('dx', 'dy', None, 'band')
All inputs are finite; a program needn't handle non-finite values.
Results may differ from a plain program's by a relative error of at most 0.000073.
Values sent between devices are 32-bit elements; how exact they have to be, the bound alone decides.
No kernel may reach another device: no remote copies, remote signals or barrier semaphores. Data moves between devices by JAX's collectives and lax.ppermute only.
A program may use at most 64 MiB of HBM per device.

v0:
```python
import jax
import jax.numpy as jnp
from jax import lax
from jax.sharding import PartitionSpec as P

DEGREE = 3
coeffs = (
    -5369.0 / 1800.0,
    12.0 / 7.0,
    -15.0 / 56.0,
    10.0 / 189.0,
    -1.0 / 112.0,
    2.0 / 1925.0,
    -1.0 / 16632.0,
)
half_width = 5.0
centre_value = 7.0


def with_halo(cells, sides, width):
    for axis, dim in sides:
        count = lax.axis_size(axis)
        head = lax.slice_in_dim(cells, 0, width, axis=dim)
        tail = lax.slice_in_dim(cells, cells.shape[dim] - width, cells.shape[dim], axis=dim)
        cells = jnp.concatenate(
            [
                lax.ppermute(tail, axis, [(i, (i + 1) % count) for i in range(count)]),
                cells,
                lax.ppermute(head, axis, [((i + 1) % count, i) for i in range(count)]),
            ],
            axis=dim,
        )
    return cells


def apply_ham(field, potential):
    padded = with_halo(field, (("dx", 0), ("dy", 1)), 6)
    size_x = field.shape[0]
    size_y = field.shape[1]
    lap = 3.0 * coeffs[0] * field
    for shift in range(1, 7):
        near = (
            padded[6 + shift : 6 + shift + size_x, 6 : 6 + size_y]
            + padded[6 - shift : 6 - shift + size_x, 6 : 6 + size_y]
        )
        near = (
            near
            + padded[6 : 6 + size_x, 6 + shift : 6 + shift + size_y]
            + padded[6 : 6 + size_x, 6 - shift : 6 - shift + size_y]
        )
        near = near + jnp.roll(field, shift, 2) + jnp.roll(field, -shift, 2)
        lap = lap + coeffs[shift] * near
    return -0.5 * lap + potential[..., None] * field


def shards(states, potential):
    prev = states
    cur = (apply_ham(states, potential) - centre_value * states) / half_width
    for step in range(1, DEGREE):
        nxt = 2.0 * (apply_ham(cur, potential) - centre_value * cur) / half_width - prev
        prev, cur = (cur, nxt)
    block = cur.shape[3]
    cells = cur.shape[0] * cur.shape[1] * cur.shape[2]
    local = cur.reshape(cells, block)
    gathered = lax.all_gather(local, "band", axis=1, tiled=True)
    total = cells * lax.axis_size("dx") * lax.axis_size("dy")
    partial_gram = (
        jnp.dot(
            gathered.T,
            gathered,
            precision=lax.Precision.HIGHEST,
            preferred_element_type=jnp.float32,
        )
        / total
    )
    correlation = lax.psum(partial_gram, ("dx", "dy"))
    factor = jnp.linalg.cholesky(correlation)
    eye = jnp.eye(correlation.shape[0], dtype=jnp.float32)
    inverse = jax.scipy.linalg.solve_triangular(factor, eye, lower=True)
    my_rows = lax.dynamic_slice_in_dim(inverse, lax.axis_index("band") * block, block, 0)
    result = jnp.dot(
        gathered, my_rows.T, precision=lax.Precision.HIGHEST, preferred_element_type=jnp.float32
    )
    return result.reshape(cur.shape)


def solution(mesh):
    return jax.shard_map(
        shards,
        mesh=mesh,
        in_specs=(P("dx", "dy", None, "band"), P("dx", "dy", None)),
        out_specs=P("dx", "dy", None, "band"),
        check_vma=False,
    )
```

profile of v0, /device:TPU:0, one launch (start us, length us, event | category | flops | bytes accessed | tf_op | source)
XLA Modules:
  0.0 442.6 jit_solution(4787194779673460491)
XLA Ops:
  19.1 3.7 collective-permute-start.2
  23.0 19.9 %collective-permute-done.2 = f32[18,6,8,256]{3,2,1,0:T(8,128)S(1)} collective-permute-done((f32[18,6,8,256]{3,2,1,0:T(8,128)S(1)}, f32[18,6,8,256]{3,2,1,0:T(8,128)S(1)}, u32[]{:S(2)}, u32[]{:S(2)}) %collective-permute-start.2) | collective-permute-done | bytes 884768 | tf_op jit(solution)/shard_map/ppermute | solution.py:29
  42.8 19.5 %collective-permute-done.3 = f32[18,6,8,256]{3,2,1,0:T(8,128)S(1)} collective-permute-done((f32[18,6,8,256]{3,2,1,0:T(8,128)S(1)}, f32[18,6,8,256]{3,2,1,0:T(8,128)S(1)}, u32[]{:S(2)}, u32[]{:S(2)}) %collective-permute-start.3) | collective-permute-done | bytes 884768 | tf_op jit(solution)/shard_map/ppermute | solution.py:27
  65.2 9.0 %collective-permute-done.4 = f32[6,8,8,256]{3,2,1,0:T(8,128)S(1)} collective-permute-done((f32[6,8,8,256]{3,2,1,0:T(8,128)S(1)}, f32[6,8,8,256]{3,2,1,0:T(8,128)S(1)}, u32[]{:S(2)}, u32[]{:S(2)}) %collective-permute-start.4) | collective-permute-done | bytes 393248 | tf_op jit(solution)/shard_map/ppermute | solution.py:29
  78.5 19.5 %collective-permute-done.6 = f32[18,6,8,256]{3,2,1,0:T(8,128)S(1)} collective-permute-done((f32[18,6,8,256]{3,2,1,0:T(8,128)S(1)}, f32[18,6,8,256]{3,2,1,0:T(8,128)S(1)}, u32[]{:S(2)}, u32[]{:S(2)}) %collective-permute-start.6) | collective-permute-done | bytes 884768 | tf_op jit(solution)/shard_map/ppermute | solution.py:29
  98.0 18.8 %collective-permute-done.7 = f32[18,6,8,256]{3,2,1,0:T(8,128)S(1)} collective-permute-done((f32[18,6,8,256]{3,2,1,0:T(8,128)S(1)}, f32[18,6,8,256]{3,2,1,0:T(8,128)S(1)}, u32[]{:S(2)}, u32[]{:S(2)}) %collective-permute-start.7) | collective-permute-done | bytes 884768 | tf_op jit(solution)/shard_map/ppermute | solution.py:27
  120.0 8.4 %collective-permute-done.8 = f32[6,8,8,256]{3,2,1,0:T(8,128)S(1)} collective-permute-done((f32[6,8,8,256]{3,2,1,0:T(8,128)S(1)}, f32[6,8,8,256]{3,2,1,0:T(8,128)S(1)}, u32[]{:S(2)}, u32[]{:S(2)}) %collective-permute-start.8) | collective-permute-done | bytes 393248 | tf_op jit(solution)/shard_map/ppermute | solution.py:29
  133.3 19.8 %collective-permute-done.10 = f32[18,6,8,256]{3,2,1,0:T(8,128)S(1)} collective-permute-done((f32[18,6,8,256]{3,2,1,0:T(8,128)S(1)}, f32[18,6,8,256]{3,2,1,0:T(8,128)S(1)}, u32[]{:S(2)}, u32[]{:S(2)}) %collective-permute-start.10) | collective-permute-done | bytes 884768 | tf_op jit(solution)/shard_map/ppermute | solution.py:29
  153.1 20.1 %collective-permute-done.11 = f32[18,6,8,256]{3,2,1,0:T(8,128)S(1)} collective-permute-done((f32[18,6,8,256]{3,2,1,0:T(8,128)S(1)}, f32[18,6,8,256]{3,2,1,0:T(8,128)S(1)}, u32[]{:S(2)}, u32[]{:S(2)}) %collective-permute-start.11) | collective-permute-done | bytes 884768 | tf_op jit(solution)/shard_map/ppermute | solution.py:27
  175.6 11.1 %all_gather.3 = f32[384,512]{1,0:T(8,128)S(1)} all-gather(f32[384,256]{1,0:T(8,128)S(1)} %bitcast.53), channel_id=1, replica_groups=mesh['dx'=4,'dy'=4,'band'=2] {'band'}, dimensions={1}, use_global_device_ids=true | all-gather | bytes 1179648 | tf_op jit(solution)/shard_map/all_gather | solution.py:65
  186.7 2.9 convolution_multiply_fusion
  190.8 92.1 %all-reduce.3.cloned.1.call-done = f32[512,512]{0,1:T(8,128)} async-done(((f32[512,512]{0,1:T(8,128)}), f32[512,512]{0,1:T(8,128)}) %all-reduce.3.cloned.1.call-update) | async-done | bytes 1048592 | tf_op jit(solution)/shard_map/psum | solution.py:76
  285.8 11.7 %cholesky.104 = f32[128,128]{1,0:T(8,128)S(1)} custom-call(f32[128,128]{1,0:T(8,128)S(1)} %cholesky.266), custom_call_target="Cholesky" | custom-call | tf_op jit(solution)/shard_map/jit(cholesky)/cholesky | solution.py:77
  297.6 9.8 %custom-call.31 = f32[1,128,128]{1,2,0:T(8,128)S(1)} custom-call(f32[1,128,128]{2,1,0:T(8,128)S(1)} %get-tuple-element.93), custom_call_target="InvertDiagBlocksLowerTriangular" | custom-call | tf_op jit(solution)/shard_map/jit(cholesky)/cholesky | solution.py:77
  310.0 11.9 %cholesky.217 = f32[128,128]{1,0:T(8,128)S(1)} custom-call(f32[128,128]{1,0:T(8,128)S(1)} %cholesky.270), custom_call_target="Cholesky" | custom-call | tf_op jit(solution)/shard_map/jit(cholesky)/cholesky | solution.py:77
  321.9 9.8 %custom-call.32 = f32[1,128,128]{1,2,0:T(8,128)S(1)} custom-call(f32[1,128,128]{2,1,0:T(8,128)S(1)} %get-tuple-element.90), custom_call_target="InvertDiagBlocksLowerTriangular" | custom-call | tf_op jit(solution)/shard_map/jit(cholesky)/cholesky | solution.py:77
  333.3 11.7 %cholesky.238 = f32[128,128]{1,0:T(8,128)S(1)} custom-call(f32[128,128]{1,0:T(8,128)S(1)} %cholesky.275), custom_call_target="Cholesky" | custom-call | tf_op jit(solution)/shard_map/jit(cholesky)/cholesky | solution.py:77
  345.7 9.8 %custom-call.33 = f32[1,128,128]{1,2,0:T(8,128)S(1)} custom-call(f32[1,128,128]{2,1,0:T(8,128)S(1)} %get-tuple-element.87), custom_call_target="InvertDiagBlocksLowerTriangular" | custom-call | tf_op jit(solution)/shard_map/jit(cholesky)/cholesky | solution.py:77
  356.9 11.9 %cholesky.255 = f32[128,128]{1,0:T(8,128)S(1)} custom-call(f32[128,128]{1,0:T(8,128)S(1)} %convolution_subtract_fusion.5), custom_call_target="Cholesky" | custom-call | tf_op jit(solution)/shard_map/jit(cholesky)/cholesky | solution.py:77
  373.9 14.1 %while.1 = (s32[]{:T(128)}, f32[512,512]{1,0:T(8,128)}, s32[4,2]{0,1:T(2,128)S(1)}, f32[4,128,128]{2,1,0:T(8,128)}, s32[]{:T(128)}) while((s32[]{:T(128)}, f32[512,512]{1,0:T(8,128)}, s32[4,2]{0,1:T(2,128)S(1)}, f32[4,128,128]{2,1,0:T(8,128)}, s32[]{:T(128)}) %tuple.58), condition=%wide.while_cond, body=%wide.while_body.sunk | while | flops 2 | bytes 132705 | solution.py:79
  374.5 2.9 bitcast_dynamic-update-slice_fusion.2
  378.1 2.9 bitcast_dynamic-update-slice_fusion.2
  381.6 2.9 bitcast_dynamic-update-slice_fusion.2
  387.9 40.1 %custom-call.34 = f32[4,128,128]{1,2,0:T(8,128)S(1)} custom-call(f32[4,128,128]{2,1,0:T(8,128)} %get-tuple-element.12), custom_call_target="InvertDiagBlocksLowerTriangular" | custom-call | tf_op jit(solution)/shard_map/jit(_solve_triangular)/triangular_solve | solution.py:79
  (104 shorter events, 55.9 us)
Async XLA Ops:
  6.5 9.9 %copy-start = (f32[6,8,8,256]{3,2,1,0:T(8,128)S(1)}, f32[6,8,8,256]{3,2,1,0:T(8,128)}, u32[]{:S(2)}) copy-start(f32[6,8,8,256]{3,2,1,0:T(8,128)} %param.2) | copy-start | bytes 1179652
  6.5 276.4 %all-reduce.3.cloned.1.call-start = ((), (), s32[]{:S(2)}) async-start(), calls=%async_computation | async-start | bytes 2097152 | tf_op jit(solution)/shard_map/psum | solution.py:76
  6.5 9.9 %collective-permute-start.1 = (f32[6,8,8,256]{3,2,1,0:T(8,128)}, f32[6,8,8,256]{3,2,1,0:T(8,128)S(1)}, u32[]{:S(2)}, u32[]{:S(2)}) collective-permute-start(f32[6,8,8,256]{3,2,1,0:T(8,128)} %param.2), channel_id=1, source_target_pairs={{0,8},{8,16},{16,24},{24,0},{1,9},{9,17},{17,25},{25,1},{2,10},{10... | collective-permute-start | bytes 1179656 | tf_op jit(solution)/shard_map/ppermute | solution.py:27
  7.0 11.8 %collective-permute-start = (f32[6,8,8,256]{3,2,1,0:T(8,128)}, f32[6,8,8,256]{3,2,1,0:T(8,128)S(1)}, u32[]{:S(2)}, u32[]{:S(2)}) collective-permute-start(f32[6,8,8,256]{3,2,1,0:T(8,128)} %param.2), channel_id=1, source_target_pairs={{8,0},{16,8},{24,16},{0,24},{9,1},{17,9},{25,17},{1,25},{10,2},{18... | collective-permute-start | bytes 1179656 | tf_op jit(solution)/shard_map/ppermute | solution.py:29
  18.9 3.9 copy-start.4
  19.1 23.7 %collective-permute-start.2 = (f32[18,6,8,256]{3,2,1,0:T(8,128)S(1)}, f32[18,6,8,256]{3,2,1,0:T(8,128)S(1)}, u32[]{:S(2)}, u32[]{:S(2)}) collective-permute-start(f32[18,6,8,256]{3,2,1,0:T(8,128)S(1)} %get-tuple-element.33), channel_id=1, source_target_pairs={{2,0},{4,2},{6,4},{0,6},{3,1},{5,3},{7,5},{1,7},{10,8},{12,10},{14... | collective-permute-start | bytes 2654216 | tf_op jit(solution)/shard_map/ppermute | solution.py:29
  22.7 39.6 %collective-permute-start.3 = (f32[18,6,8,256]{3,2,1,0:T(8,128)S(1)}, f32[18,6,8,256]{3,2,1,0:T(8,128)S(1)}, u32[]{:S(2)}, u32[]{:S(2)}) collective-permute-start(f32[18,6,8,256]{3,2,1,0:T(8,128)S(1)} %get-tuple-element.34), channel_id=1, source_target_pairs={{0,2},{2,4},{4,6},{6,0},{1,3},{3,5},{5,7},{7,1},{8,10},{10,12},{12... | collective-permute-start | bytes 2654216 | tf_op jit(solution)/shard_map/ppermute | solution.py:27
  64.3 9.9 %collective-permute-start.4 = (f32[6,8,8,256]{3,2,1,0:T(8,128)S(1)}, f32[6,8,8,256]{3,2,1,0:T(8,128)S(1)}, u32[]{:S(2)}, u32[]{:S(2)}) collective-permute-start(f32[6,8,8,256]{3,2,1,0:T(8,128)S(1)} %get-tuple-element.21), channel_id=1, source_target_pairs={{8,0},{16,8},{24,16},{0,24},{9,1},{17,9},{25,17},{1,25},{10,2},{18... | collective-permute-start | bytes 1179656 | tf_op jit(solution)/shard_map/ppermute | solution.py:29
  65.0 10.8 %collective-permute-start.5 = (f32[6,8,8,256]{3,2,1,0:T(8,128)S(1)}, f32[6,8,8,256]{3,2,1,0:T(8,128)S(1)}, u32[]{:S(2)}, u32[]{:S(2)}) collective-permute-start(f32[6,8,8,256]{3,2,1,0:T(8,128)S(1)} %get-tuple-element.21), channel_id=1, source_target_pairs={{0,8},{8,16},{16,24},{24,0},{1,9},{9,17},{17,25},{25,1},{2,10},{10... | collective-permute-start | bytes 1179656 | tf_op jit(solution)/shard_map/ppermute | solution.py:27
  76.1 21.8 %collective-permute-start.6 = (f32[18,6,8,256]{3,2,1,0:T(8,128)S(1)}, f32[18,6,8,256]{3,2,1,0:T(8,128)S(1)}, u32[]{:S(2)}, u32[]{:S(2)}) collective-permute-start(f32[18,6,8,256]{3,2,1,0:T(8,128)S(1)} %get-tuple-element.31), channel_id=1, source_target_pairs={{2,0},{4,2},{6,4},{0,6},{3,1},{5,3},{7,5},{1,7},{10,8},{12,10},{14... | collective-permute-start | bytes 2654216 | tf_op jit(solution)/shard_map/ppermute | solution.py:29
  77.9 38.8 %collective-permute-start.7 = (f32[18,6,8,256]{3,2,1,0:T(8,128)S(1)}, f32[18,6,8,256]{3,2,1,0:T(8,128)S(1)}, u32[]{:S(2)}, u32[]{:S(2)}) collective-permute-start(f32[18,6,8,256]{3,2,1,0:T(8,128)S(1)} %get-tuple-element.32), channel_id=1, source_target_pairs={{0,2},{2,4},{4,6},{6,0},{1,3},{3,5},{5,7},{7,1},{8,10},{10,12},{12... | collective-permute-start | bytes 2654216 | tf_op jit(solution)/shard_map/ppermute | solution.py:27
  119.2 9.2 %collective-permute-start.8 = (f32[6,8,8,256]{3,2,1,0:T(8,128)S(1)}, f32[6,8,8,256]{3,2,1,0:T(8,128)S(1)}, u32[]{:S(2)}, u32[]{:S(2)}) collective-permute-start(f32[6,8,8,256]{3,2,1,0:T(8,128)S(1)} %fusion.29), channel_id=1, source_target_pairs={{8,0},{16,8},{24,16},{0,24},{9,1},{17,9},{25,17},{1,25},{10,2},{18... | collective-permute-start | bytes 1179656 | tf_op jit(solution)/shard_map/ppermute | solution.py:29
  119.2 10.8 %collective-permute-start.9 = (f32[6,8,8,256]{3,2,1,0:T(8,128)S(1)}, f32[6,8,8,256]{3,2,1,0:T(8,128)S(1)}, u32[]{:S(2)}, u32[]{:S(2)}) collective-permute-start(f32[6,8,8,256]{3,2,1,0:T(8,128)S(1)} %fusion.29), channel_id=1, source_target_pairs={{0,8},{8,16},{16,24},{24,0},{1,9},{9,17},{17,25},{25,1},{2,10},{10... | collective-permute-start | bytes 1179656 | tf_op jit(solution)/shard_map/ppermute | solution.py:27
  130.4 22.7 %collective-permute-start.10 = (f32[18,6,8,256]{3,2,1,0:T(8,128)S(1)}, f32[18,6,8,256]{3,2,1,0:T(8,128)S(1)}, u32[]{:S(2)}, u32[]{:S(2)}) collective-permute-start(f32[18,6,8,256]{3,2,1,0:T(8,128)S(1)} %get-tuple-element.27), channel_id=1, source_target_pairs={{2,0},{4,2},{6,4},{0,6},{3,1},{5,3},{7,5},{1,7},{10,8},{12,10},{14... | collective-permute-start | bytes 2654216 | tf_op jit(solution)/shard_map/ppermute | solution.py:29
  133.0 40.2 %collective-permute-start.11 = (f32[18,6,8,256]{3,2,1,0:T(8,128)S(1)}, f32[18,6,8,256]{3,2,1,0:T(8,128)S(1)}, u32[]{:S(2)}, u32[]{:S(2)}) collective-permute-start(f32[18,6,8,256]{3,2,1,0:T(8,128)S(1)} %get-tuple-element.28), channel_id=1, source_target_pairs={{0,2},{2,4},{4,6},{6,0},{1,3},{3,5},{5,7},{7,1},{8,10},{10,12},{12... | collective-permute-start | bytes 2654216 | tf_op jit(solution)/shard_map/ppermute | solution.py:27
  282.9 1.7 copy-start.1
  284.8 1.0 copy-start.3
  345.0 83.4 %copy-start.2 = (f32[512,512]{1,0:T(8,128)S(1)}, f32[512,512]{1,0:T(8,128)}, u32[]{:S(2)}) copy-start(f32[512,512]{1,0:T(8,128)} %fusion.157) | copy-start | bytes 3145732
Sparse Core Ops, SparseCore 0:
  189.7 93.1 all-reduce.2
where the time goes:
time: 449 us; the launch traced here: 443 us
  waiting for transfers between devices  235 us (52%)
  other arithmetic  128 us (29%)
  local copies, waits for them, and re-layouts  23.5 us (5%)
  between operations  16.6 us (4%)
  matrix products  15.7 us (3%)
  starting transfers between devices  12 us (3%)
  blocking collectives  11.1 us (2%)
    psum x1, waiting for transfers between devices, shards(): correlation = lax.psum(partial_gram, ('dx', 'dy'))  92.1 us
    another operation x14, other arithmetic, shards(): factor = jnp.linalg.cholesky(correlation)  78.8 us
    ppermute x6, waiting for transfers between devices, with_halo(): lax.ppermute(head, axis, [((i + 1) % count, i) for i in range(count)])  78.7 us
    ppermute x6, waiting for transfers between devices, with_halo(): lax.ppermute(tail, axis, [(i, (i + 1) % count) for i in range(count)])  64.4 us
    another operation x3, other arithmetic, shards(): inverse = jax.scipy.linalg.solve_triangular(factor, eye, lower=True)  41.2 us
    another operation x12, local copies, waits for them, and re-layouts  14.1 us
    all_gather x1, blocking collectives, shards(): gathered = lax.all_gather(local, 'band', axis=1, tiled=True)  11.1 us
    ppermute x6, starting transfers between devices, with_halo(): lax.ppermute(head, axis, [((i + 1) % count, i) for i in range(count)])  10.8 us
  transfers between devices with their start and end apart: 13, of which 13 were waited for; matrix products, arithmetic and copies ran while one was open for 2% of the time, Pallas kernels for 0%

commit v1 on v0

--- a/solution.py
+++ b/solution.py
@@ -73,7 +73,7 @@
         )
         / total
     )
-    correlation = lax.psum(partial_gram, ("dx", "dy"))
+    correlation = jnp.sum(lax.all_gather(partial_gram, ("dx", "dy")), axis=0)
     factor = jnp.linalg.cholesky(correlation)
     eye = jnp.eye(correlation.shape[0], dtype=jnp.float32)
     inverse = jax.scipy.linalg.solve_triangular(factor, eye, lower=True)

time: 449 us -> 488 us (1.087)
  waiting for transfers between devices: 235 us -> 268 us
  other arithmetic: 128 us -> 136 us
    all_gather x0 -> x1, waiting for transfers between devices: none -> 125 us  [shards(): correlation = jnp.sum(lax.all_gather(partial_gram, ('dx', 'dy')), axis=0)]
    psum x1 -> x0, waiting for transfers between devices: 92.1 us -> none  [shards(): correlation = lax.psum(partial_gram, ('dx', 'dy'))]
    reduce_sum x0 -> x1, other arithmetic: none -> 7.91 us  [shards(): correlation = jnp.sum(lax.all_gather(partial_gram, ('dx', 'dy')), axis=0)]
  transfers between devices with their start and end apart: 13 -> 13, of which waited for: 13 -> 13; matrix products, arithmetic and copies ran while one was open for 2% -> 1% of each run, Pallas kernels for 0% -> 0%
where the time goes in v1:
time: 488 us; the launch traced here: 482 us
  waiting for transfers between devices  268 us (55%)
  other arithmetic  136 us (28%)
  local copies, waits for them, and re-layouts  22 us (5%)
  between operations  16.6 us (3%)
  matrix products  15.9 us (3%)
  starting transfers between devices  12 us (2%)
  blocking collectives  11.1 us (2%)
    all_gather x1, waiting for transfers between devices, shards(): correlation = jnp.sum(lax.all_gather(partial_gram, ('dx', 'dy')), axis=0)  125 us
    ppermute x6, waiting for transfers between devices, with_halo(): lax.ppermute(head, axis, [((i + 1) % count, i) for i in range(count)])  78.7 us
    another operation x14, other arithmetic, shards(): factor = jnp.linalg.cholesky(correlation)  78.6 us
    ppermute x6, waiting for transfers between devices, with_halo(): lax.ppermute(tail, axis, [(i, (i + 1) % count) for i in range(count)])  64.4 us
    another operation x3, other arithmetic, shards(): inverse = jax.scipy.linalg.solve_triangular(factor, eye, lower=True)  41.2 us
    another operation x12, local copies, waits for them, and re-layouts  13.9 us
    all_gather x1, blocking collectives, shards(): gathered = lax.all_gather(local, 'band', axis=1, tiled=True)  11.1 us
    ppermute x6, starting transfers between devices, with_halo(): lax.ppermute(head, axis, [((i + 1) % count, i) for i in range(count)])  10.8 us
  transfers between devices with their start and end apart: 13, of which 13 were waited for; matrix products, arithmetic and copies ran while one was open for 1% of the time, Pallas kernels for 0%

profile of v1, /device:TPU:0, one launch (start us, length us, event | category | flops | bytes accessed | tf_op | source)
XLA Modules:
  0.0 481.7 jit_solution(6598609146694521677)
XLA Ops:
  19.1 3.7 collective-permute-start.2
  23.0 19.9 %collective-permute-done.2 = f32[18,6,8,256]{3,2,1,0:T(8,128)S(1)} collective-permute-done((f32[18,6,8,256]{3,2,1,0:T(8,128)S(1)}, f32[18,6,8,256]{3,2,1,0:T(8,128)S(1)}, u32[]{:S(2)}, u32[]{:S(2)}) %collective-permute-start.2) | collective-permute-done | bytes 884768 | tf_op jit(solution)/shard_map/ppermute | solution.py:29
  42.8 19.5 %collective-permute-done.3 = f32[18,6,8,256]{3,2,1,0:T(8,128)S(1)} collective-permute-done((f32[18,6,8,256]{3,2,1,0:T(8,128)S(1)}, f32[18,6,8,256]{3,2,1,0:T(8,128)S(1)}, u32[]{:S(2)}, u32[]{:S(2)}) %collective-permute-start.3) | collective-permute-done | bytes 884768 | tf_op jit(solution)/shard_map/ppermute | solution.py:27
  65.2 9.0 %collective-permute-done.4 = f32[6,8,8,256]{3,2,1,0:T(8,128)S(1)} collective-permute-done((f32[6,8,8,256]{3,2,1,0:T(8,128)S(1)}, f32[6,8,8,256]{3,2,1,0:T(8,128)S(1)}, u32[]{:S(2)}, u32[]{:S(2)}) %collective-permute-start.4) | collective-permute-done | bytes 393248 | tf_op jit(solution)/shard_map/ppermute | solution.py:29
  78.5 19.5 %collective-permute-done.6 = f32[18,6,8,256]{3,2,1,0:T(8,128)S(1)} collective-permute-done((f32[18,6,8,256]{3,2,1,0:T(8,128)S(1)}, f32[18,6,8,256]{3,2,1,0:T(8,128)S(1)}, u32[]{:S(2)}, u32[]{:S(2)}) %collective-permute-start.6) | collective-permute-done | bytes 884768 | tf_op jit(solution)/shard_map/ppermute | solution.py:29
  98.0 18.8 %collective-permute-done.7 = f32[18,6,8,256]{3,2,1,0:T(8,128)S(1)} collective-permute-done((f32[18,6,8,256]{3,2,1,0:T(8,128)S(1)}, f32[18,6,8,256]{3,2,1,0:T(8,128)S(1)}, u32[]{:S(2)}, u32[]{:S(2)}) %collective-permute-start.7) | collective-permute-done | bytes 884768 | tf_op jit(solution)/shard_map/ppermute | solution.py:27
  120.0 8.4 %collective-permute-done.8 = f32[6,8,8,256]{3,2,1,0:T(8,128)S(1)} collective-permute-done((f32[6,8,8,256]{3,2,1,0:T(8,128)S(1)}, f32[6,8,8,256]{3,2,1,0:T(8,128)S(1)}, u32[]{:S(2)}, u32[]{:S(2)}) %collective-permute-start.8) | collective-permute-done | bytes 393248 | tf_op jit(solution)/shard_map/ppermute | solution.py:29
  133.3 19.8 %collective-permute-done.10 = f32[18,6,8,256]{3,2,1,0:T(8,128)S(1)} collective-permute-done((f32[18,6,8,256]{3,2,1,0:T(8,128)S(1)}, f32[18,6,8,256]{3,2,1,0:T(8,128)S(1)}, u32[]{:S(2)}, u32[]{:S(2)}) %collective-permute-start.10) | collective-permute-done | bytes 884768 | tf_op jit(solution)/shard_map/ppermute | solution.py:29
  153.1 20.1 %collective-permute-done.11 = f32[18,6,8,256]{3,2,1,0:T(8,128)S(1)} collective-permute-done((f32[18,6,8,256]{3,2,1,0:T(8,128)S(1)}, f32[18,6,8,256]{3,2,1,0:T(8,128)S(1)}, u32[]{:S(2)}, u32[]{:S(2)}) %collective-permute-start.11) | collective-permute-done | bytes 884768 | tf_op jit(solution)/shard_map/ppermute | solution.py:27
  175.6 11.1 %all_gather.9 = f32[384,512]{1,0:T(8,128)S(1)} all-gather(f32[384,256]{1,0:T(8,128)S(1)} %bitcast.55), channel_id=1, replica_groups=mesh['dx'=4,'dy'=4,'band'=2] {'band'}, dimensions={1}, use_global_device_ids=true | all-gather | bytes 1179648 | tf_op jit(solution)/shard_map/all_gather | solution.py:65
  190.8 124.8 %all-gather.3.cloned.1.call-done = f32[8192,512]{1,0:T(8,128)} async-done(((f32[512,512]{1,0:T(8,128)}), f32[8192,512]{1,0:T(8,128)}) %all-gather.3.cloned.1.call-update) | async-done | bytes 16777232 | tf_op jit(solution)/shard_map/all_gather | solution.py:76
  315.6 7.9 %reduce_sum.9 = f32[512,512]{1,0:T(8,128)S(1)} reduce(f32[16,512,512]{2,1,0:T(8,128)} %bitcast.54, f32[]{:T(128)} %constant.179.clone.1), dimensions={0}, to_apply=%region_0.1 | reduce | flops 3932160 | bytes 17825796 | tf_op jit(solution)/shard_map/reduce_sum | solution.py:76
  325.0 11.7 %cholesky.104 = f32[128,128]{1,0:T(8,128)S(1)} custom-call(f32[128,128]{1,0:T(8,128)S(1)} %cholesky.266), custom_call_target="Cholesky" | custom-call | tf_op jit(solution)/shard_map/jit(cholesky)/cholesky | solution.py:77
  336.9 9.8 %custom-call.31 = f32[1,128,128]{1,2,0:T(8,128)S(1)} custom-call(f32[1,128,128]{2,1,0:T(8,128)S(1)} %get-tuple-element.93), custom_call_target="InvertDiagBlocksLowerTriangular" | custom-call | tf_op jit(solution)/shard_map/jit(cholesky)/cholesky | solution.py:77
  349.3 11.9 %cholesky.217 = f32[128,128]{1,0:T(8,128)S(1)} custom-call(f32[128,128]{1,0:T(8,128)S(1)} %cholesky.270), custom_call_target="Cholesky" | custom-call | tf_op jit(solution)/shard_map/jit(cholesky)/cholesky | solution.py:77
  361.2 9.8 %custom-call.32 = f32[1,128,128]{1,2,0:T(8,128)S(1)} custom-call(f32[1,128,128]{2,1,0:T(8,128)S(1)} %get-tuple-element.90), custom_call_target="InvertDiagBlocksLowerTriangular" | custom-call | tf_op jit(solution)/shard_map/jit(cholesky)/cholesky | solution.py:77
  372.5 11.7 %cholesky.238 = f32[128,128]{1,0:T(8,128)S(1)} custom-call(f32[128,128]{1,0:T(8,128)S(1)} %cholesky.275), custom_call_target="Cholesky" | custom-call | tf_op jit(solution)/shard_map/jit(cholesky)/cholesky | solution.py:77
  384.9 9.8 %custom-call.33 = f32[1,128,128]{1,2,0:T(8,128)S(1)} custom-call(f32[1,128,128]{2,1,0:T(8,128)S(1)} %get-tuple-element.87), custom_call_target="InvertDiagBlocksLowerTriangular" | custom-call | tf_op jit(solution)/shard_map/jit(cholesky)/cholesky | solution.py:77
  396.4 11.7 %cholesky.255 = f32[128,128]{1,0:T(8,128)S(1)} custom-call(f32[128,128]{1,0:T(8,128)S(1)} %convolution_subtract_fusion.5), custom_call_target="Cholesky" | custom-call | tf_op jit(solution)/shard_map/jit(cholesky)/cholesky | solution.py:77
  413.1 13.9 %while.1 = (s32[]{:T(128)}, f32[512,512]{1,0:T(8,128)}, s32[4,2]{0,1:T(2,128)S(1)}, f32[4,128,128]{2,1,0:T(8,128)}, s32[]{:T(128)}) while((s32[]{:T(128)}, f32[512,512]{1,0:T(8,128)}, s32[4,2]{0,1:T(2,128)S(1)}, f32[4,128,128]{2,1,0:T(8,128)}, s32[]{:T(128)}) %tuple.58), condition=%wide.while_cond, body=%wide.while_body.sunk | while | flops 2 | bytes 132705 | solution.py:79
  413.8 2.8 bitcast_dynamic-update-slice_fusion.2
  417.3 2.8 bitcast_dynamic-update-slice_fusion.2
  420.7 2.8 bitcast_dynamic-update-slice_fusion.2
  427.0 40.1 %custom-call.34 = f32[4,128,128]{1,2,0:T(8,128)S(1)} custom-call(f32[4,128,128]{2,1,0:T(8,128)} %get-tuple-element.12), custom_call_target="InvertDiagBlocksLowerTriangular" | custom-call | tf_op jit(solution)/shard_map/jit(_solve_triangular)/triangular_solve | solution.py:79
  (103 shorter events, 57.6 us)
Async XLA Ops:
  6.5 9.9 %copy-start = (f32[6,8,8,256]{3,2,1,0:T(8,128)S(1)}, f32[6,8,8,256]{3,2,1,0:T(8,128)}, u32[]{:S(2)}) copy-start(f32[6,8,8,256]{3,2,1,0:T(8,128)} %param.2) | copy-start | bytes 1179652
  6.5 309.0 %all-gather.3.cloned.1.call-start = ((), (), s32[]{:S(2)}) async-start(), calls=%async_computation | async-start | bytes 17825792 | tf_op jit(solution)/shard_map/all_gather | solution.py:76
  6.5 9.9 %collective-permute-start.1 = (f32[6,8,8,256]{3,2,1,0:T(8,128)}, f32[6,8,8,256]{3,2,1,0:T(8,128)S(1)}, u32[]{:S(2)}, u32[]{:S(2)}) collective-permute-start(f32[6,8,8,256]{3,2,1,0:T(8,128)} %param.2), channel_id=1, source_target_pairs={{0,8},{8,16},{16,24},{24,0},{1,9},{9,17},{17,25},{25,1},{2,10},{10... | collective-permute-start | bytes 1179656 | tf_op jit(solution)/shard_map/ppermute | solution.py:27
  7.0 11.8 %collective-permute-start = (f32[6,8,8,256]{3,2,1,0:T(8,128)}, f32[6,8,8,256]{3,2,1,0:T(8,128)S(1)}, u32[]{:S(2)}, u32[]{:S(2)}) collective-permute-start(f32[6,8,8,256]{3,2,1,0:T(8,128)} %param.2), channel_id=1, source_target_pairs={{8,0},{16,8},{24,16},{0,24},{9,1},{17,9},{25,17},{1,25},{10,2},{18... | collective-permute-start | bytes 1179656 | tf_op jit(solution)/shard_map/ppermute | solution.py:29
  18.9 3.9 copy-start.3
  19.1 23.7 %collective-permute-start.2 = (f32[18,6,8,256]{3,2,1,0:T(8,128)S(1)}, f32[18,6,8,256]{3,2,1,0:T(8,128)S(1)}, u32[]{:S(2)}, u32[]{:S(2)}) collective-permute-start(f32[18,6,8,256]{3,2,1,0:T(8,128)S(1)} %get-tuple-element.33), channel_id=1, source_target_pairs={{2,0},{4,2},{6,4},{0,6},{3,1},{5,3},{7,5},{1,7},{10,8},{12,10},{14... | collective-permute-start | bytes 2654216 | tf_op jit(solution)/shard_map/ppermute | solution.py:29
  22.7 39.6 %collective-permute-start.3 = (f32[18,6,8,256]{3,2,1,0:T(8,128)S(1)}, f32[18,6,8,256]{3,2,1,0:T(8,128)S(1)}, u32[]{:S(2)}, u32[]{:S(2)}) collective-permute-start(f32[18,6,8,256]{3,2,1,0:T(8,128)S(1)} %get-tuple-element.34), channel_id=1, source_target_pairs={{0,2},{2,4},{4,6},{6,0},{1,3},{3,5},{5,7},{7,1},{8,10},{10,12},{12... | collective-permute-start | bytes 2654216 | tf_op jit(solution)/shard_map/ppermute | solution.py:27
  64.3 9.9 %collective-permute-start.4 = (f32[6,8,8,256]{3,2,1,0:T(8,128)S(1)}, f32[6,8,8,256]{3,2,1,0:T(8,128)S(1)}, u32[]{:S(2)}, u32[]{:S(2)}) collective-permute-start(f32[6,8,8,256]{3,2,1,0:T(8,128)S(1)} %get-tuple-element.21), channel_id=1, source_target_pairs={{8,0},{16,8},{24,16},{0,24},{9,1},{17,9},{25,17},{1,25},{10,2},{18... | collective-permute-start | bytes 1179656 | tf_op jit(solution)/shard_map/ppermute | solution.py:29
  65.0 10.8 %collective-permute-start.5 = (f32[6,8,8,256]{3,2,1,0:T(8,128)S(1)}, f32[6,8,8,256]{3,2,1,0:T(8,128)S(1)}, u32[]{:S(2)}, u32[]{:S(2)}) collective-permute-start(f32[6,8,8,256]{3,2,1,0:T(8,128)S(1)} %get-tuple-element.21), channel_id=1, source_target_pairs={{0,8},{8,16},{16,24},{24,0},{1,9},{9,17},{17,25},{25,1},{2,10},{10... | collective-permute-start | bytes 1179656 | tf_op jit(solution)/shard_map/ppermute | solution.py:27
  76.1 21.8 %collective-permute-start.6 = (f32[18,6,8,256]{3,2,1,0:T(8,128)S(1)}, f32[18,6,8,256]{3,2,1,0:T(8,128)S(1)}, u32[]{:S(2)}, u32[]{:S(2)}) collective-permute-start(f32[18,6,8,256]{3,2,1,0:T(8,128)S(1)} %get-tuple-element.31), channel_id=1, source_target_pairs={{2,0},{4,2},{6,4},{0,6},{3,1},{5,3},{7,5},{1,7},{10,8},{12,10},{14... | collective-permute-start | bytes 2654216 | tf_op jit(solution)/shard_map/ppermute | solution.py:29
  77.9 38.8 %collective-permute-start.7 = (f32[18,6,8,256]{3,2,1,0:T(8,128)S(1)}, f32[18,6,8,256]{3,2,1,0:T(8,128)S(1)}, u32[]{:S(2)}, u32[]{:S(2)}) collective-permute-start(f32[18,6,8,256]{3,2,1,0:T(8,128)S(1)} %get-tuple-element.32), channel_id=1, source_target_pairs={{0,2},{2,4},{4,6},{6,0},{1,3},{3,5},{5,7},{7,1},{8,10},{10,12},{12... | collective-permute-start | bytes 2654216 | tf_op jit(solution)/shard_map/ppermute | solution.py:27
  119.2 9.2 %collective-permute-start.8 = (f32[6,8,8,256]{3,2,1,0:T(8,128)S(1)}, f32[6,8,8,256]{3,2,1,0:T(8,128)S(1)}, u32[]{:S(2)}, u32[]{:S(2)}) collective-permute-start(f32[6,8,8,256]{3,2,1,0:T(8,128)S(1)} %fusion.29), channel_id=1, source_target_pairs={{8,0},{16,8},{24,16},{0,24},{9,1},{17,9},{25,17},{1,25},{10,2},{18... | collective-permute-start | bytes 1179656 | tf_op jit(solution)/shard_map/ppermute | solution.py:29
  119.2 10.8 %collective-permute-start.9 = (f32[6,8,8,256]{3,2,1,0:T(8,128)S(1)}, f32[6,8,8,256]{3,2,1,0:T(8,128)S(1)}, u32[]{:S(2)}, u32[]{:S(2)}) collective-permute-start(f32[6,8,8,256]{3,2,1,0:T(8,128)S(1)} %fusion.29), channel_id=1, source_target_pairs={{0,8},{8,16},{16,24},{24,0},{1,9},{9,17},{17,25},{25,1},{2,10},{10... | collective-permute-start | bytes 1179656 | tf_op jit(solution)/shard_map/ppermute | solution.py:27
  130.4 22.7 %collective-permute-start.10 = (f32[18,6,8,256]{3,2,1,0:T(8,128)S(1)}, f32[18,6,8,256]{3,2,1,0:T(8,128)S(1)}, u32[]{:S(2)}, u32[]{:S(2)}) collective-permute-start(f32[18,6,8,256]{3,2,1,0:T(8,128)S(1)} %get-tuple-element.27), channel_id=1, source_target_pairs={{2,0},{4,2},{6,4},{0,6},{3,1},{5,3},{7,5},{1,7},{10,8},{12,10},{14... | collective-permute-start | bytes 2654216 | tf_op jit(solution)/shard_map/ppermute | solution.py:29
  133.0 40.2 %collective-permute-start.11 = (f32[18,6,8,256]{3,2,1,0:T(8,128)S(1)}, f32[18,6,8,256]{3,2,1,0:T(8,128)S(1)}, u32[]{:S(2)}, u32[]{:S(2)}) collective-permute-start(f32[18,6,8,256]{3,2,1,0:T(8,128)S(1)} %get-tuple-element.28), channel_id=1, source_target_pairs={{0,2},{2,4},{4,6},{6,0},{1,3},{3,5},{5,7},{7,1},{8,10},{10,12},{12... | collective-permute-start | bytes 2654216 | tf_op jit(solution)/shard_map/ppermute | solution.py:27
  324.0 1.0 copy-start.2
  384.3 83.2 %copy-start.1 = (f32[512,512]{1,0:T(8,128)S(1)}, f32[512,512]{1,0:T(8,128)}, u32[]{:S(2)}) copy-start(f32[512,512]{1,0:T(8,128)} %fusion.157) | copy-start | bytes 3145732
Sparse Core Ops, SparseCore 0:
  189.7 125.8 all-gather.2
